TPU v7x, 128 devices: a whole 4x4x4 slice. The times are simulated.
128 devices in a mesh: chan: 2 (over x_hi), blk: 64 (over y, z, x_lo, core).
Axes of the slice: x: 4 (x_hi: 2, x_lo: 2; x = x_hi * 2 + x_lo), y: 4, z: 4, core: 2. Of those that a mesh axis runs over, the one named last changes fastest.
Arguments:
- features: bfloat16 [64, 2, 256, 128], P('blk', 'chan'), may hold values from -6 to 6
- transforms: bfloat16 [8, 128, 128], replicated, may hold values from -0.5 to 0.5
- self_weight: bfloat16 [128, 128], replicated, may hold values from -0.5 to 0.5
- tile_rows: int32 [8, 64, 64, 8], P('chan', 'blk'), may hold values from 0 to 3
- tile_cols: int32 [8, 64, 64, 8], P('chan', 'blk'), may hold values from 0 to 3
- tile_ids: int32 [8, 64, 64, 8], P('chan', 'blk'), may hold values from 0 to 31
- tile_count: int32 [8, 64, 64], P('chan', 'blk'), may hold values from 0 to 8
- tile_pool: bfloat16 [8, 64, 32, 128, 128], P('chan', 'blk'), may hold values from -0.0234375 to 0.0234375
Outputs:
- updated: bfloat16 [64, 2, 256, 128], P('blk', 'chan')
All inputs are finite; a program needn't handle non-finite values.
Results may differ from a plain program's by a relative error of at most 0.0041.
Values may be sent and summed in bfloat16 or wider, within the bound.
No kernel may reach another device: no remote copies, remote signals or barrier semaphores. Data moves between devices by JAX's collectives and lax.ppermute only.
A program may use at most 128 MiB of HBM per device.

v0:
```python
import math
import jax
import jax.numpy as jnp
from jax import lax
from jax.sharding import PartitionSpec as P


def shards(
    features, transforms, self_weight, tile_rows, tile_cols, tile_ids, tile_count, tile_pool
):
    chan_count = lax.axis_size("chan")
    chan_index = lax.axis_index("chan")
    own_rows = features[0, 0]
    half_rows = own_rows.shape[0]
    width = own_rows.shape[1]
    tile_size = tile_pool.shape[-1]
    pool_size = tile_pool.shape[2]
    block_rows = half_rows * chan_count
    tiles_block = block_rows // tile_size
    rel_dev = transforms.shape[0] // chan_count
    slot_count = tile_rows.shape[-1]
    rows_list = tile_rows[:, 0]
    cols_list = tile_cols[:, 0]
    ids_list = tile_ids[:, 0]
    count_list = tile_count[:, 0]
    pool_flat = tile_pool[:, 0].reshape(rel_dev, pool_size, tile_size * tile_size)
    slot_range = jnp.arange(slot_count)
    tile_range = jnp.arange(tiles_block)
    pool_range = jnp.arange(pool_size)

    def apply_group(total, hidden_group, first):
        group = hidden_group.shape[1]
        cols_now = lax.dynamic_slice_in_dim(cols_list, first, group, 1)
        rows_now = lax.dynamic_slice_in_dim(rows_list, first, group, 1)
        ids_now = lax.dynamic_slice_in_dim(ids_list, first, group, 1)
        count_now = lax.dynamic_slice_in_dim(count_list, first, group, 1)
        pick_cols = (cols_now[..., None] == tile_range).astype(jnp.bfloat16)
        flat_hidden = hidden_group.reshape(rel_dev, group, tiles_block, tile_size * width)
        picked = jnp.einsum(
            "rgks,rgsx->rgkx", pick_cols, flat_hidden, preferred_element_type=jnp.float32
        ).astype(jnp.bfloat16)
        picked = picked.reshape(rel_dev, group, slot_count, tile_size, width)
        pick_ids = (ids_now[..., None] == pool_range).astype(jnp.bfloat16)
        weights = jnp.einsum(
            "rgkp,rpx->rgkx", pick_ids, pool_flat, preferred_element_type=jnp.float32
        ).astype(jnp.bfloat16)
        weights = weights.reshape(rel_dev, group, slot_count, tile_size, tile_size)
        product = jnp.einsum(
            "rgkab,rgkbd->rgkad", weights, picked, preferred_element_type=jnp.float32
        )
        live = (slot_range < count_now[..., None]).astype(jnp.float32)
        onehot = (rows_now[..., None] == tile_range).astype(jnp.float32) * live[..., None]
        return total + jnp.einsum(
            "rgkt,rgkad->tad", onehot, product, precision=lax.Precision.HIGHEST
        )

    empty = jnp.zeros((tiles_block, tile_size, width), jnp.float32)
    all_hidden = jnp.einsum(
        "nd,rde->rne", own_rows, transforms, preferred_element_type=jnp.float32
    ).astype(jnp.bfloat16)
    mine = lax.all_to_all(all_hidden, "chan", split_axis=0, concat_axis=1, tiled=True)
    piece = lax.all_gather(mine, "blk", axis=1, tiled=True)
    blocks_here = piece.shape[1] // block_rows

    def fetch(offset, group):
        part_rows = lax.dynamic_slice_in_dim(piece, offset * block_rows, group * block_rows, 1)
        return part_rows.reshape(rel_dev, group, tiles_block, tile_size, width)

    group = math.gcd(blocks_here, 4)
    turns = blocks_here // group

    def step_once(turn, carry):
        return apply_group(carry, fetch(turn * group, group), turn * group)

    agg = lax.fori_loop(0, turns, step_once, empty)
    partial_rows = agg.reshape(block_rows, width)
    summed = lax.psum(partial_rows, "chan")
    share = lax.dynamic_slice_in_dim(summed, chan_index * half_rows, half_rows, 0)
    selfterm = jnp.dot(own_rows, self_weight, preferred_element_type=jnp.float32)
    updated = jax.nn.relu(selfterm + share).astype(jnp.bfloat16)
    return updated.reshape(1, 1, half_rows, width)


def solution(mesh):
    placed = (
        P("blk", "chan", None, None),
        P(),
        P(),
        P("chan", "blk", None, None),
        P("chan", "blk", None, None),
        P("chan", "blk", None, None),
        P("chan", "blk", None),
        P("chan", "blk", None, None, None),
    )
    return jax.shard_map(
        shards, mesh=mesh, in_specs=placed, out_specs=P("blk", "chan", None, None), check_vma=False
    )
```

profile of v0, /device:TPU:1, one launch (start us, length us, event | category | flops | bytes accessed | tf_op | source)
XLA Modules:
  0.0 706.5 jit_solution(2026471395278241592)
XLA Ops:
  8.7 13.2 %all_to_all.18 = bf16[8,256,128]{1,2,0:T(8,128)(2,1)S(1)} all-to-all(bf16[8,256,128]{1,2,0:T(8,128)(2,1)S(1)} %fusion.31), channel_id=1, replica_groups=mesh['chan'=2,'blk'=64] {'chan'}, dimensions={0} | all-to-all | bytes 1048576 | tf_op jit(solution)/shard_map/all_to_all | solution.py:61
  23.0 7.3 %reshape_squeeze.3 = bf16[4,32,16384]{2,1,0:T(8,128)(2,1)} reshape(bf16[4,1,32,128,128]{4,3,2,1,0:T(8,128)(2,1)} %param.17) | data formatting | bytes 8388608 | tf_op jit(solution)/shard_map/reshape;squeeze | solution.py:26
  30.8 181.1 %all-gather.2.cloned.1.call-done = bf16[4,32768,128]{2,1,0:T(8,128)(2,1)} async-done(((bf16[4,512,128]{2,1,0:T(8,128)(2,1)}), bf16[4,32768,128]{2,1,0:T(8,128)(2,1)}) %all-gather.2.cloned.1.call-update) | async-done | bytes 33554448 | tf_op jit(solution)/shard_map/all_gather | solution.py:62
  211.9 453.9 %while.17 = (s32[]{:T(128)}, f32[4,128,128]{2,0,1:T(4,128)S(1)}, s32[4,64,8]{2,0,1:T(4,128)S(1)}, s32[4,64]{0,1:T(8,128)S(1)}, s32[4,64,8]{2,1,0:T(8,128)S(1)}, ...) while((s32[]{:T(128)}, f32[4,128,128]{2,0,1:T(4,128)S(1)}, ...), condition=%wide.region_1.0_spmd.clone.clone, body=%wide.region_0.0_spmd.clone.clone.sunk | while | flops 792860416 | bytes 65542100 | solution.py:75
  211.9 3.1 constant_dynamic-slice_fusion.9
  214.9 2.6 reshape.58
  221.1 4.5 fusion.61
  225.6 14.6 %fusion.63 = f32[4,128,128]{2,0,1:T(4,128)S(1)} fusion(f32[4,4,8,128,128]{4,3,2,1,0:T(8,128)} %fusion.61, f32[4,128,128]{2,0,1:T(4,128)S(1)} %get-tuple-element.418, pred[]{:T(512)S(6)} %compare.3, f32[4,4,8]{2,0,1:T(4,128)S(1)} %fusion.62, s32[4,4,8]{2,0,1:T(4,128)S(1)} %get-tuple-element.402), kind=kOutput, calls=%fused_computation.14.clone.1 | convolution fusion | flops 100795392 | bytes 8913921 | tf_op jit(solution)/shard_map/while/body/eval_jaxpr/rgkt,rgkad->tad/dot_general | solution.py:53
  240.2 3.1 constant_dynamic-slice_fusion.9
  243.3 2.6 reshape.58
  249.4 4.5 fusion.61
  254.0 14.6 %fusion.63 = f32[4,128,128]{2,0,1:T(4,128)S(1)} fusion(f32[4,4,8,128,128]{4,3,2,1,0:T(8,128)} %fusion.61, f32[4,128,128]{2,0,1:T(4,128)S(1)} %get-tuple-element.418, pred[]{:T(512)S(6)} %compare.3, f32[4,4,8]{2,0,1:T(4,128)S(1)} %fusion.62, s32[4,4,8]{2,0,1:T(4,128)S(1)} %get-tuple-element.402), kind=kOutput, calls=%fused_computation.14.clone.1 | convolution fusion | flops 100795392 | bytes 8913921 | tf_op jit(solution)/shard_map/while/body/eval_jaxpr/rgkt,rgkad->tad/dot_general | solution.py:53
  268.6 3.1 constant_dynamic-slice_fusion.9
  271.7 2.6 reshape.58
  277.8 4.5 fusion.61
  282.3 14.6 %fusion.63 = f32[4,128,128]{2,0,1:T(4,128)S(1)} fusion(f32[4,4,8,128,128]{4,3,2,1,0:T(8,128)} %fusion.61, f32[4,128,128]{2,0,1:T(4,128)S(1)} %get-tuple-element.418, pred[]{:T(512)S(6)} %compare.3, f32[4,4,8]{2,0,1:T(4,128)S(1)} %fusion.62, s32[4,4,8]{2,0,1:T(4,128)S(1)} %get-tuple-element.402), kind=kOutput, calls=%fused_computation.14.clone.1 | convolution fusion | flops 100795392 | bytes 8913921 | tf_op jit(solution)/shard_map/while/body/eval_jaxpr/rgkt,rgkad->tad/dot_general | solution.py:53
  297.0 3.1 constant_dynamic-slice_fusion.9
  300.1 2.6 reshape.58
  306.2 4.5 fusion.61
  310.7 14.6 %fusion.63 = f32[4,128,128]{2,0,1:T(4,128)S(1)} fusion(f32[4,4,8,128,128]{4,3,2,1,0:T(8,128)} %fusion.61, f32[4,128,128]{2,0,1:T(4,128)S(1)} %get-tuple-element.418, pred[]{:T(512)S(6)} %compare.3, f32[4,4,8]{2,0,1:T(4,128)S(1)} %fusion.62, s32[4,4,8]{2,0,1:T(4,128)S(1)} %get-tuple-element.402), kind=kOutput, calls=%fused_computation.14.clone.1 | convolution fusion | flops 100795392 | bytes 8913921 | tf_op jit(solution)/shard_map/while/body/eval_jaxpr/rgkt,rgkad->tad/dot_general | solution.py:53
  325.4 3.1 constant_dynamic-slice_fusion.9
  328.4 2.6 reshape.58
  334.5 4.5 fusion.61
  339.1 14.6 %fusion.63 = f32[4,128,128]{2,0,1:T(4,128)S(1)} fusion(f32[4,4,8,128,128]{4,3,2,1,0:T(8,128)} %fusion.61, f32[4,128,128]{2,0,1:T(4,128)S(1)} %get-tuple-element.418, pred[]{:T(512)S(6)} %compare.3, f32[4,4,8]{2,0,1:T(4,128)S(1)} %fusion.62, s32[4,4,8]{2,0,1:T(4,128)S(1)} %get-tuple-element.402), kind=kOutput, calls=%fused_computation.14.clone.1 | convolution fusion | flops 100795392 | bytes 8913921 | tf_op jit(solution)/shard_map/while/body/eval_jaxpr/rgkt,rgkad->tad/dot_general | solution.py:53
  353.7 3.1 constant_dynamic-slice_fusion.9
  356.8 2.6 reshape.58
  362.9 4.5 fusion.61
  367.5 14.6 %fusion.63 = f32[4,128,128]{2,0,1:T(4,128)S(1)} fusion(f32[4,4,8,128,128]{4,3,2,1,0:T(8,128)} %fusion.61, f32[4,128,128]{2,0,1:T(4,128)S(1)} %get-tuple-element.418, pred[]{:T(512)S(6)} %compare.3, f32[4,4,8]{2,0,1:T(4,128)S(1)} %fusion.62, s32[4,4,8]{2,0,1:T(4,128)S(1)} %get-tuple-element.402), kind=kOutput, calls=%fused_computation.14.clone.1 | convolution fusion | flops 100795392 | bytes 8913921 | tf_op jit(solution)/shard_map/while/body/eval_jaxpr/rgkt,rgkad->tad/dot_general | solution.py:53
  382.1 3.1 constant_dynamic-slice_fusion.9
  385.2 2.6 reshape.58
  391.3 4.5 fusion.61
  395.8 14.6 %fusion.63 = f32[4,128,128]{2,0,1:T(4,128)S(1)} fusion(f32[4,4,8,128,128]{4,3,2,1,0:T(8,128)} %fusion.61, f32[4,128,128]{2,0,1:T(4,128)S(1)} %get-tuple-element.418, pred[]{:T(512)S(6)} %compare.3, f32[4,4,8]{2,0,1:T(4,128)S(1)} %fusion.62, s32[4,4,8]{2,0,1:T(4,128)S(1)} %get-tuple-element.402), kind=kOutput, calls=%fused_computation.14.clone.1 | convolution fusion | flops 100795392 | bytes 8913921 | tf_op jit(solution)/shard_map/while/body/eval_jaxpr/rgkt,rgkad->tad/dot_general | solution.py:53
  410.5 3.1 constant_dynamic-slice_fusion.9
  413.5 2.6 reshape.58
  419.7 4.5 fusion.61
  424.2 14.6 %fusion.63 = f32[4,128,128]{2,0,1:T(4,128)S(1)} fusion(f32[4,4,8,128,128]{4,3,2,1,0:T(8,128)} %fusion.61, f32[4,128,128]{2,0,1:T(4,128)S(1)} %get-tuple-element.418, pred[]{:T(512)S(6)} %compare.3, f32[4,4,8]{2,0,1:T(4,128)S(1)} %fusion.62, s32[4,4,8]{2,0,1:T(4,128)S(1)} %get-tuple-element.402), kind=kOutput, calls=%fused_computation.14.clone.1 | convolution fusion | flops 100795392 | bytes 8913921 | tf_op jit(solution)/shard_map/while/body/eval_jaxpr/rgkt,rgkad->tad/dot_general | solution.py:53
  438.8 3.1 constant_dynamic-slice_fusion.9
  441.9 2.6 reshape.58
  448.0 4.5 fusion.61
  452.6 14.6 %fusion.63 = f32[4,128,128]{2,0,1:T(4,128)S(1)} fusion(f32[4,4,8,128,128]{4,3,2,1,0:T(8,128)} %fusion.61, f32[4,128,128]{2,0,1:T(4,128)S(1)} %get-tuple-element.418, pred[]{:T(512)S(6)} %compare.3, f32[4,4,8]{2,0,1:T(4,128)S(1)} %fusion.62, s32[4,4,8]{2,0,1:T(4,128)S(1)} %get-tuple-element.402), kind=kOutput, calls=%fused_computation.14.clone.1 | convolution fusion | flops 100795392 | bytes 8913921 | tf_op jit(solution)/shard_map/while/body/eval_jaxpr/rgkt,rgkad->tad/dot_general | solution.py:53
  467.2 3.1 constant_dynamic-slice_fusion.9
  470.3 2.6 reshape.58
  476.4 4.5 fusion.61
  480.9 14.6 %fusion.63 = f32[4,128,128]{2,0,1:T(4,128)S(1)} fusion(f32[4,4,8,128,128]{4,3,2,1,0:T(8,128)} %fusion.61, f32[4,128,128]{2,0,1:T(4,128)S(1)} %get-tuple-element.418, pred[]{:T(512)S(6)} %compare.3, f32[4,4,8]{2,0,1:T(4,128)S(1)} %fusion.62, s32[4,4,8]{2,0,1:T(4,128)S(1)} %get-tuple-element.402), kind=kOutput, calls=%fused_computation.14.clone.1 | convolution fusion | flops 100795392 | bytes 8913921 | tf_op jit(solution)/shard_map/while/body/eval_jaxpr/rgkt,rgkad->tad/dot_general | solution.py:53
  495.6 3.1 constant_dynamic-slice_fusion.9
  498.6 2.6 reshape.58
  504.8 4.5 fusion.61
  509.3 14.6 %fusion.63 = f32[4,128,128]{2,0,1:T(4,128)S(1)} fusion(f32[4,4,8,128,128]{4,3,2,1,0:T(8,128)} %fusion.61, f32[4,128,128]{2,0,1:T(4,128)S(1)} %get-tuple-element.418, pred[]{:T(512)S(6)} %compare.3, f32[4,4,8]{2,0,1:T(4,128)S(1)} %fusion.62, s32[4,4,8]{2,0,1:T(4,128)S(1)} %get-tuple-element.402), kind=kOutput, calls=%fused_computation.14.clone.1 | convolution fusion | flops 100795392 | bytes 8913921 | tf_op jit(solution)/shard_map/while/body/eval_jaxpr/rgkt,rgkad->tad/dot_general | solution.py:53
  524.0 3.1 constant_dynamic-slice_fusion.9
  533.1 4.5 fusion.61
  537.7 14.6 %fusion.63 = f32[4,128,128]{2,0,1:T(4,128)S(1)} fusion(f32[4,4,8,128,128]{4,3,2,1,0:T(8,128)} %fusion.61, f32[4,128,128]{2,0,1:T(4,128)S(1)} %get-tuple-element.418, pred[]{:T(512)S(6)} %compare.3, f32[4,4,8]{2,0,1:T(4,128)S(1)} %fusion.62, s32[4,4,8]{2,0,1:T(4,128)S(1)} %get-tuple-element.402), kind=kOutput, calls=%fused_computation.14.clone.1 | convolution fusion | flops 100795392 | bytes 8913921 | tf_op jit(solution)/shard_map/while/body/eval_jaxpr/rgkt,rgkad->tad/dot_general | solution.py:53
  552.3 3.1 constant_dynamic-slice_fusion.9
  561.5 4.5 fusion.61
  566.0 14.6 %fusion.63 = f32[4,128,128]{2,0,1:T(4,128)S(1)} fusion(f32[4,4,8,128,128]{4,3,2,1,0:T(8,128)} %fusion.61, f32[4,128,128]{2,0,1:T(4,128)S(1)} %get-tuple-element.418, pred[]{:T(512)S(6)} %compare.3, f32[4,4,8]{2,0,1:T(4,128)S(1)} %fusion.62, s32[4,4,8]{2,0,1:T(4,128)S(1)} %get-tuple-element.402), kind=kOutput, calls=%fused_computation.14.clone.1 | convolution fusion | flops 100795392 | bytes 8913921 | tf_op jit(solution)/shard_map/while/body/eval_jaxpr/rgkt,rgkad->tad/dot_general | solution.py:53
  580.7 3.1 constant_dynamic-slice_fusion.9
  589.9 4.5 fusion.61
  594.4 14.6 %fusion.63 = f32[4,128,128]{2,0,1:T(4,128)S(1)} fusion(f32[4,4,8,128,128]{4,3,2,1,0:T(8,128)} %fusion.61, f32[4,128,128]{2,0,1:T(4,128)S(1)} %get-tuple-element.418, pred[]{:T(512)S(6)} %compare.3, f32[4,4,8]{2,0,1:T(4,128)S(1)} %fusion.62, s32[4,4,8]{2,0,1:T(4,128)S(1)} %get-tuple-element.402), kind=kOutput, calls=%fused_computation.14.clone.1 | convolution fusion | flops 100795392 | bytes 8913921 | tf_op jit(solution)/shard_map/while/body/eval_jaxpr/rgkt,rgkad->tad/dot_general | solution.py:53
  609.1 3.1 constant_dynamic-slice_fusion.9
  618.2 4.5 fusion.61
  622.8 14.6 %fusion.63 = f32[4,128,128]{2,0,1:T(4,128)S(1)} fusion(f32[4,4,8,128,128]{4,3,2,1,0:T(8,128)} %fusion.61, f32[4,128,128]{2,0,1:T(4,128)S(1)} %get-tuple-element.418, pred[]{:T(512)S(6)} %compare.3, f32[4,4,8]{2,0,1:T(4,128)S(1)} %fusion.62, s32[4,4,8]{2,0,1:T(4,128)S(1)} %get-tuple-element.402), kind=kOutput, calls=%fused_computation.14.clone.1 | convolution fusion | flops 100795392 | bytes 8913921 | tf_op jit(solution)/shard_map/while/body/eval_jaxpr/rgkt,rgkad->tad/dot_general | solution.py:53
  637.4 3.1 constant_dynamic-slice_fusion.9
  646.6 4.5 fusion.61
  651.2 14.6 %fusion.63 = f32[4,128,128]{2,0,1:T(4,128)S(1)} fusion(f32[4,4,8,128,128]{4,3,2,1,0:T(8,128)} %fusion.61, f32[4,128,128]{2,0,1:T(4,128)S(1)} %get-tuple-element.418, pred[]{:T(512)S(6)} %compare.3, f32[4,4,8]{2,0,1:T(4,128)S(1)} %fusion.62, s32[4,4,8]{2,0,1:T(4,128)S(1)} %get-tuple-element.402), kind=kOutput, calls=%fused_computation.14.clone.1 | convolution fusion | flops 100795392 | bytes 8913921 | tf_op jit(solution)/shard_map/while/body/eval_jaxpr/rgkt,rgkad->tad/dot_general | solution.py:53
  666.5 31.5 %all-reduce.2.cloned.1.call-done = f32[512,128]{1,0:T(8,128)} async-done(((f32[512,128]{1,0:T(8,128)}), f32[512,128]{1,0:T(8,128)}) %all-reduce.2.cloned.1.call-update) | async-done | bytes 262160 | tf_op jit(solution)/shard_map/psum | solution.py:77
  (160 shorter events, 75.9 us)
Async XLA Ops:
  6.5 1.0 copy-start
  6.5 205.3 %all-gather.2.cloned.1.call-start = ((), (), s32[]{:S(2)}) async-start(), calls=%async_computation.1 | async-start | bytes 34078720 | tf_op jit(solution)/shard_map/all_gather | solution.py:62
  22.9 675.1 %all-reduce.2.cloned.1.call-start = ((), (), s32[]{:S(2)}) async-start(), calls=%async_computation.2 | async-start | bytes 524288 | tf_op jit(solution)/shard_map/psum | solution.py:77
  22.9 7.4 %copy-start.4 = (s32[4,1,64,8]{2,3,1,0:T(8,128)S(1)}, s32[4,1,64,8]{2,3,1,0:T(8,128)}, u32[]{:S(2)}) copy-start(s32[4,1,64,8]{2,3,1,0:T(8,128)} %param.13) | copy-start | bytes 24580
  23.0 7.5 %copy-start.5 = (s32[4,1,64,8]{2,3,1,0:T(8,128)S(1)}, s32[4,1,64,8]{2,3,1,0:T(8,128)}, u32[]{:S(2)}) copy-start(s32[4,1,64,8]{2,3,1,0:T(8,128)} %param.15) | copy-start | bytes 24580
  23.0 7.6 %copy-start.6 = (s32[4,1,64,8]{2,3,1,0:T(8,128)S(1)}, s32[4,1,64,8]{2,3,1,0:T(8,128)}, u32[]{:S(2)}) copy-start(s32[4,1,64,8]{2,3,1,0:T(8,128)} %param.14) | copy-start | bytes 24580
  23.0 7.7 %copy-start.7 = (s32[4,1,64]{2,1,0:T(1,128)S(1)}, s32[4,1,64]{2,1,0:T(1,128)}, u32[]{:S(2)}) copy-start(s32[4,1,64]{2,1,0:T(1,128)} %param.16) | copy-start | bytes 3076
  211.8 486.1 %copy-start.2 = (bf16[1,1,256,128]{3,2,1,0:T(8,128)(2,1)S(1)}, bf16[1,1,256,128]{3,2,1,0:T(8,128)(2,1)}, u32[]{:S(2)}) copy-start(bf16[1,1,256,128]{3,2,1,0:T(8,128)(2,1)} %param.10) | copy-start | bytes 196612
  211.9 486.1 %copy-start.3 = (bf16[128,128]{1,0:T(8,128)(2,1)S(1)}, bf16[128,128]{1,0:T(8,128)(2,1)}, u32[]{:S(2)}) copy-start(bf16[128,128]{1,0:T(8,128)(2,1)} %param.12) | copy-start | bytes 98308
  217.6 2.2 copy-start.1
  245.9 2.2 copy-start.1
  274.3 2.2 copy-start.1
  302.7 2.2 copy-start.1
  331.1 2.2 copy-start.1
  359.4 2.2 copy-start.1
  387.8 2.2 copy-start.1
  416.2 2.2 copy-start.1
  444.5 2.2 copy-start.1
  472.9 2.2 copy-start.1
  501.3 2.2 copy-start.1
  529.6 2.2 copy-start.1
  558.0 2.2 copy-start.1
  586.4 2.2 copy-start.1
  614.8 2.2 copy-start.1
  643.1 2.2 copy-start.1
Sparse Core Ops, SparseCore 0:
  23.0 188.7 all-gather.1
  666.6 31.2 all-reduce.1
where the time goes:
time: 709 us; the launch traced here: 706 us
  matrix products  357 us (50%)
  waiting for transfers between devices  213 us (30%)
  local copies, waits for them, and re-layouts  108 us (15%)
  between operations  13.5 us (2%)
  blocking collectives  13.2 us (2%)
    dot_general x16, matrix products, apply_group(): jnp.einsum('rgkt,rgkad->tad', onehot, product, precision=lax.Precision.HI...  233 us
    all_gather x1, waiting for transfers between devices, shards(): piece = lax.all_gather(mine, 'blk', axis=1, tiled=True)  181 us
    dot_general x16, matrix products, apply_group(): jnp.einsum('rgkab,rgkbd->rgkad', weights, picked, preferred_element_type=...  71.4 us
    dynamic_slice x16, local copies, waits for them, and re-layouts, fetch(): lax.dynamic_slice_in_dim(piece, offset * block_rows, group * block_rows, 1)  49 us
    reshape x16, local copies, waits for them, and re-layouts, apply_group(): hidden_group.reshape(rel_dev, group, tiles_block, tile_size * width)  42 us
    psum x1, waiting for transfers between devices, shards(): summed = lax.psum(partial_rows, 'chan')  31.5 us
    dot_general x16, matrix products, apply_group(): jnp.einsum('rgks,rgsx->rgkx', pick_cols, flat_hidden, preferred_element_t...  28.2 us
    dot_general x16, matrix products, apply_group(): jnp.einsum('rgkp,rpx->rgkx', pick_ids, pool_flat, preferred_element_type=...  20.7 us
  transfers between devices with their start and end apart: 2, of which 2 were waited for; matrix products, arithmetic and copies ran while one was open for 1% of the time, Pallas kernels for 0%

commit v1 on v0

--- a/solution.py
+++ b/solution.py
@@ -59,7 +59,9 @@
         "nd,rde->rne", own_rows, transforms, preferred_element_type=jnp.float32
     ).astype(jnp.bfloat16)
     mine = lax.all_to_all(all_hidden, "chan", split_axis=0, concat_axis=1, tiled=True)
-    piece = lax.all_gather(mine, "blk", axis=1, tiled=True)
+    piece = jnp.concatenate(
+        lax.all_to_all(jnp.stack([mine] * lax.axis_size("blk")), "blk", 0, 0), axis=1
+    )
     blocks_here = piece.shape[1] // block_rows
 
     def fetch(offset, group):

time: 709 us -> 1070 us (1.51)
  waiting for transfers between devices: 213 us -> 531 us
  local copies, waits for them, and re-layouts: 108 us -> 142 us
    all_to_all x0 -> x1, waiting for transfers between devices: none -> 430 us  [shards(): lax.all_to_all(jnp.stack([mine] * lax.axis_size('blk')), 'blk', 0, 0)]
    all_gather x1 -> x0, waiting for transfers between devices: 181 us -> none  [shards(): piece = lax.all_gather(mine, 'blk', axis=1, tiled=True)]
    psum x1, waiting for transfers between devices: 31.5 us -> 100 us  [shards(): summed = lax.psum(partial_rows, 'chan')]
    all_to_all x0 -> x1, local copies, waits for them, and re-layouts: none -> 23 us  [shards(): lax.all_to_all(jnp.stack([mine] * lax.axis_size('blk')), 'blk', 0, 0)]
    another operation x0 -> x1, local copies, waits for them, and re-layouts: none -> 11.3 us  [shards(): jnp.stack([mine] * lax.axis_size('blk'))]
where the time goes in v1:
time: 1070 us
  waiting for transfers between devices  531 us (50%)
  matrix products  357 us (33%)
  local copies, waits for them, and re-layouts  142 us (13%)
  between operations  13.5 us (1%)
  blocking collectives  13.2 us (1%)
    all_to_all x1, waiting for transfers between devices, shards(): lax.all_to_all(jnp.stack([mine] * lax.axis_size('blk')), 'blk', 0, 0)  430 us
    dot_general x16, matrix products, apply_group(): jnp.einsum('rgkt,rgkad->tad', onehot, product, precision=lax.Precision.HI...  233 us
    psum x1, waiting for transfers between devices, shards(): summed = lax.psum(partial_rows, 'chan')  100 us
    dot_general x16, matrix products, apply_group(): jnp.einsum('rgkab,rgkbd->rgkad', weights, picked, preferred_element_type=...  71.4 us
    dynamic_slice x16, local copies, waits for them, and re-layouts, fetch(): lax.dynamic_slice_in_dim(piece, offset * block_rows, group * block_rows, 1)  49 us
    reshape x16, local copies, waits for them, and re-layouts, apply_group(): hidden_group.reshape(rel_dev, group, tiles_block, tile_size * width)  42 us
    dot_general x16, matrix products, apply_group(): jnp.einsum('rgks,rgsx->rgkx', pick_cols, flat_hidden, preferred_element_t...  28.2 us
    all_to_all x1, local copies, waits for them, and re-layouts, shards(): lax.all_to_all(jnp.stack([mine] * lax.axis_size('blk')), 'blk', 0, 0)  23 us
  transfers between devices with their start and end apart: 2, of which 2 were waited for; matrix products, arithmetic and copies ran while one was open for 1% of the time, Pallas kernels for 0%

profile of v1, /device:TPU:1, one launch (start us, length us, event | category | flops | bytes accessed | tf_op | source)
XLA Modules:
  0.0 1068.8 jit_solution(7793653117662679595)
XLA Ops:
  8.7 13.2 %all_to_all.20 = bf16[8,256,128]{1,2,0:T(8,128)(2,1)S(1)} all-to-all(bf16[8,256,128]{1,2,0:T(8,128)(2,1)S(1)} %fusion.31), channel_id=1, replica_groups=mesh['chan'=2,'blk'=64] {'chan'}, dimensions={0} | all-to-all | bytes 1048576 | tf_op jit(solution)/shard_map/all_to_all | solution.py:61
  22.1 11.3 %stack.5 = bf16[64,4,512,128]{3,2,1,0:T(8,128)(2,1)} broadcast(bf16[4,512,128]{2,1,0:T(8,128)(2,1)S(1)} %bitcast.63), dimensions={1,2,3} | broadcast | bytes 34078720 | tf_op jit(solution)/shard_map/stack | solution.py:63
  33.5 10.6 all-to-all-start.1
  44.2 7.3 reshape_squeeze.3
  52.0 430.4 %all-to-all-done.1 = bf16[64,4,512,128]{3,2,1,0:T(8,128)(2,1)} async-done(((bf16[64,4,512,128]{3,2,1,0:T(8,128)(2,1)}), bf16[64,4,512,128]{3,2,1,0:T(8,128)(2,1)}, u32[]{:S(2)}, u32[]{:S(2)}) %all-to-all-start.1) | async-done | bytes 33554464 | tf_op jit(solution)/shard_map/all_to_all | solution.py:63
  482.4 23.0 %copy.45 = bf16[64,4,512,128]{3,2,0,1:T(8,128)(2,1)} copy(bf16[64,4,512,128]{3,2,1,0:T(8,128)(2,1)} %all-to-all-done.1) | data formatting | bytes 67108864 | tf_op jit(solution)/shard_map/all_to_all | solution.py:63
  505.4 453.9 %while.17 = (s32[]{:T(128)}, f32[4,128,128]{2,0,1:T(4,128)S(1)}, s32[4,64,8]{2,0,1:T(4,128)S(1)}, s32[4,64]{0,1:T(8,128)S(1)}, s32[4,64,8]{2,1,0:T(8,128)S(1)}, ...) while((s32[]{:T(128)}, f32[4,128,128]{2,0,1:T(4,128)S(1)}, ...), condition=%wide.region_1.0_spmd.clone.clone, body=%wide.region_0.0_spmd.clone.clone.sunk | while | flops 792860416 | bytes 65542100 | solution.py:77
  505.4 3.1 constant_dynamic-slice_fusion.9
  508.5 2.6 reshape.69
  514.6 4.5 fusion.61
  519.1 14.6 %fusion.63 = f32[4,128,128]{2,0,1:T(4,128)S(1)} fusion(f32[4,4,8,128,128]{4,3,2,1,0:T(8,128)} %fusion.61, f32[4,128,128]{2,0,1:T(4,128)S(1)} %get-tuple-element.418, pred[]{:T(512)S(6)} %compare.3, f32[4,4,8]{2,0,1:T(4,128)S(1)} %fusion.62, s32[4,4,8]{2,0,1:T(4,128)S(1)} %get-tuple-element.402), kind=kOutput, calls=%fused_computation.14.clone.1 | convolution fusion | flops 100795392 | bytes 8913921 | tf_op jit(solution)/shard_map/while/body/eval_jaxpr/rgkt,rgkad->tad/dot_general | solution.py:53
  533.8 3.1 constant_dynamic-slice_fusion.9
  536.8 2.6 reshape.69
  542.9 4.5 fusion.61
  547.5 14.6 %fusion.63 = f32[4,128,128]{2,0,1:T(4,128)S(1)} fusion(f32[4,4,8,128,128]{4,3,2,1,0:T(8,128)} %fusion.61, f32[4,128,128]{2,0,1:T(4,128)S(1)} %get-tuple-element.418, pred[]{:T(512)S(6)} %compare.3, f32[4,4,8]{2,0,1:T(4,128)S(1)} %fusion.62, s32[4,4,8]{2,0,1:T(4,128)S(1)} %get-tuple-element.402), kind=kOutput, calls=%fused_computation.14.clone.1 | convolution fusion | flops 100795392 | bytes 8913921 | tf_op jit(solution)/shard_map/while/body/eval_jaxpr/rgkt,rgkad->tad/dot_general | solution.py:53
  562.1 3.1 constant_dynamic-slice_fusion.9
  565.2 2.6 reshape.69
  571.3 4.5 fusion.61
  575.9 14.6 %fusion.63 = f32[4,128,128]{2,0,1:T(4,128)S(1)} fusion(f32[4,4,8,128,128]{4,3,2,1,0:T(8,128)} %fusion.61, f32[4,128,128]{2,0,1:T(4,128)S(1)} %get-tuple-element.418, pred[]{:T(512)S(6)} %compare.3, f32[4,4,8]{2,0,1:T(4,128)S(1)} %fusion.62, s32[4,4,8]{2,0,1:T(4,128)S(1)} %get-tuple-element.402), kind=kOutput, calls=%fused_computation.14.clone.1 | convolution fusion | flops 100795392 | bytes 8913921 | tf_op jit(solution)/shard_map/while/body/eval_jaxpr/rgkt,rgkad->tad/dot_general | solution.py:53
  590.5 3.1 constant_dynamic-slice_fusion.9
  593.6 2.6 reshape.69
  599.7 4.5 fusion.61
  604.2 14.6 %fusion.63 = f32[4,128,128]{2,0,1:T(4,128)S(1)} fusion(f32[4,4,8,128,128]{4,3,2,1,0:T(8,128)} %fusion.61, f32[4,128,128]{2,0,1:T(4,128)S(1)} %get-tuple-element.418, pred[]{:T(512)S(6)} %compare.3, f32[4,4,8]{2,0,1:T(4,128)S(1)} %fusion.62, s32[4,4,8]{2,0,1:T(4,128)S(1)} %get-tuple-element.402), kind=kOutput, calls=%fused_computation.14.clone.1 | convolution fusion | flops 100795392 | bytes 8913921 | tf_op jit(solution)/shard_map/while/body/eval_jaxpr/rgkt,rgkad->tad/dot_general | solution.py:53
  618.9 3.1 constant_dynamic-slice_fusion.9
  621.9 2.6 reshape.69
  628.1 4.5 fusion.61
  632.6 14.6 %fusion.63 = f32[4,128,128]{2,0,1:T(4,128)S(1)} fusion(f32[4,4,8,128,128]{4,3,2,1,0:T(8,128)} %fusion.61, f32[4,128,128]{2,0,1:T(4,128)S(1)} %get-tuple-element.418, pred[]{:T(512)S(6)} %compare.3, f32[4,4,8]{2,0,1:T(4,128)S(1)} %fusion.62, s32[4,4,8]{2,0,1:T(4,128)S(1)} %get-tuple-element.402), kind=kOutput, calls=%fused_computation.14.clone.1 | convolution fusion | flops 100795392 | bytes 8913921 | tf_op jit(solution)/shard_map/while/body/eval_jaxpr/rgkt,rgkad->tad/dot_general | solution.py:53
  647.2 3.1 constant_dynamic-slice_fusion.9
  650.3 2.6 reshape.69
  656.4 4.5 fusion.61
  661.0 14.6 %fusion.63 = f32[4,128,128]{2,0,1:T(4,128)S(1)} fusion(f32[4,4,8,128,128]{4,3,2,1,0:T(8,128)} %fusion.61, f32[4,128,128]{2,0,1:T(4,128)S(1)} %get-tuple-element.418, pred[]{:T(512)S(6)} %compare.3, f32[4,4,8]{2,0,1:T(4,128)S(1)} %fusion.62, s32[4,4,8]{2,0,1:T(4,128)S(1)} %get-tuple-element.402), kind=kOutput, calls=%fused_computation.14.clone.1 | convolution fusion | flops 100795392 | bytes 8913921 | tf_op jit(solution)/shard_map/while/body/eval_jaxpr/rgkt,rgkad->tad/dot_general | solution.py:53
  675.6 3.1 constant_dynamic-slice_fusion.9
  684.8 4.5 fusion.61
  689.3 14.6 %fusion.63 = f32[4,128,128]{2,0,1:T(4,128)S(1)} fusion(f32[4,4,8,128,128]{4,3,2,1,0:T(8,128)} %fusion.61, f32[4,128,128]{2,0,1:T(4,128)S(1)} %get-tuple-element.418, pred[]{:T(512)S(6)} %compare.3, f32[4,4,8]{2,0,1:T(4,128)S(1)} %fusion.62, s32[4,4,8]{2,0,1:T(4,128)S(1)} %get-tuple-element.402), kind=kOutput, calls=%fused_computation.14.clone.1 | convolution fusion | flops 100795392 | bytes 8913921 | tf_op jit(solution)/shard_map/while/body/eval_jaxpr/rgkt,rgkad->tad/dot_general | solution.py:53
  704.0 3.1 constant_dynamic-slice_fusion.9
  713.2 4.5 fusion.61
  717.7 14.6 %fusion.63 = f32[4,128,128]{2,0,1:T(4,128)S(1)} fusion(f32[4,4,8,128,128]{4,3,2,1,0:T(8,128)} %fusion.61, f32[4,128,128]{2,0,1:T(4,128)S(1)} %get-tuple-element.418, pred[]{:T(512)S(6)} %compare.3, f32[4,4,8]{2,0,1:T(4,128)S(1)} %fusion.62, s32[4,4,8]{2,0,1:T(4,128)S(1)} %get-tuple-element.402), kind=kOutput, calls=%fused_computation.14.clone.1 | convolution fusion | flops 100795392 | bytes 8913921 | tf_op jit(solution)/shard_map/while/body/eval_jaxpr/rgkt,rgkad->tad/dot_general | solution.py:53
  732.4 3.1 constant_dynamic-slice_fusion.9
  735.4 2.6 reshape.69
  741.5 4.5 fusion.61
  746.1 14.6 %fusion.63 = f32[4,128,128]{2,0,1:T(4,128)S(1)} fusion(f32[4,4,8,128,128]{4,3,2,1,0:T(8,128)} %fusion.61, f32[4,128,128]{2,0,1:T(4,128)S(1)} %get-tuple-element.418, pred[]{:T(512)S(6)} %compare.3, f32[4,4,8]{2,0,1:T(4,128)S(1)} %fusion.62, s32[4,4,8]{2,0,1:T(4,128)S(1)} %get-tuple-element.402), kind=kOutput, calls=%fused_computation.14.clone.1 | convolution fusion | flops 100795392 | bytes 8913921 | tf_op jit(solution)/shard_map/while/body/eval_jaxpr/rgkt,rgkad->tad/dot_general | solution.py:53
  760.7 3.1 constant_dynamic-slice_fusion.9
  769.9 4.5 fusion.61
  774.5 14.6 %fusion.63 = f32[4,128,128]{2,0,1:T(4,128)S(1)} fusion(f32[4,4,8,128,128]{4,3,2,1,0:T(8,128)} %fusion.61, f32[4,128,128]{2,0,1:T(4,128)S(1)} %get-tuple-element.418, pred[]{:T(512)S(6)} %compare.3, f32[4,4,8]{2,0,1:T(4,128)S(1)} %fusion.62, s32[4,4,8]{2,0,1:T(4,128)S(1)} %get-tuple-element.402), kind=kOutput, calls=%fused_computation.14.clone.1 | convolution fusion | flops 100795392 | bytes 8913921 | tf_op jit(solution)/shard_map/while/body/eval_jaxpr/rgkt,rgkad->tad/dot_general | solution.py:53
  789.1 3.1 constant_dynamic-slice_fusion.9
  798.3 4.5 fusion.61
  802.8 14.6 %fusion.63 = f32[4,128,128]{2,0,1:T(4,128)S(1)} fusion(f32[4,4,8,128,128]{4,3,2,1,0:T(8,128)} %fusion.61, f32[4,128,128]{2,0,1:T(4,128)S(1)} %get-tuple-element.418, pred[]{:T(512)S(6)} %compare.3, f32[4,4,8]{2,0,1:T(4,128)S(1)} %fusion.62, s32[4,4,8]{2,0,1:T(4,128)S(1)} %get-tuple-element.402), kind=kOutput, calls=%fused_computation.14.clone.1 | convolution fusion | flops 100795392 | bytes 8913921 | tf_op jit(solution)/shard_map/while/body/eval_jaxpr/rgkt,rgkad->tad/dot_general | solution.py:53
  817.5 3.1 constant_dynamic-slice_fusion.9
  820.5 2.6 reshape.69
  826.7 4.5 fusion.61
  831.2 14.6 %fusion.63 = f32[4,128,128]{2,0,1:T(4,128)S(1)} fusion(f32[4,4,8,128,128]{4,3,2,1,0:T(8,128)} %fusion.61, f32[4,128,128]{2,0,1:T(4,128)S(1)} %get-tuple-element.418, pred[]{:T(512)S(6)} %compare.3, f32[4,4,8]{2,0,1:T(4,128)S(1)} %fusion.62, s32[4,4,8]{2,0,1:T(4,128)S(1)} %get-tuple-element.402), kind=kOutput, calls=%fused_computation.14.clone.1 | convolution fusion | flops 100795392 | bytes 8913921 | tf_op jit(solution)/shard_map/while/body/eval_jaxpr/rgkt,rgkad->tad/dot_general | solution.py:53
  845.8 3.1 constant_dynamic-slice_fusion.9
  855.0 4.5 fusion.61
  859.6 14.6 %fusion.63 = f32[4,128,128]{2,0,1:T(4,128)S(1)} fusion(f32[4,4,8,128,128]{4,3,2,1,0:T(8,128)} %fusion.61, f32[4,128,128]{2,0,1:T(4,128)S(1)} %get-tuple-element.418, pred[]{:T(512)S(6)} %compare.3, f32[4,4,8]{2,0,1:T(4,128)S(1)} %fusion.62, s32[4,4,8]{2,0,1:T(4,128)S(1)} %get-tuple-element.402), kind=kOutput, calls=%fused_computation.14.clone.1 | convolution fusion | flops 100795392 | bytes 8913921 | tf_op jit(solution)/shard_map/while/body/eval_jaxpr/rgkt,rgkad->tad/dot_general | solution.py:53
  874.2 3.1 constant_dynamic-slice_fusion.9
  883.4 4.5 fusion.61
  887.9 14.6 %fusion.63 = f32[4,128,128]{2,0,1:T(4,128)S(1)} fusion(f32[4,4,8,128,128]{4,3,2,1,0:T(8,128)} %fusion.61, f32[4,128,128]{2,0,1:T(4,128)S(1)} %get-tuple-element.418, pred[]{:T(512)S(6)} %compare.3, f32[4,4,8]{2,0,1:T(4,128)S(1)} %fusion.62, s32[4,4,8]{2,0,1:T(4,128)S(1)} %get-tuple-element.402), kind=kOutput, calls=%fused_computation.14.clone.1 | convolution fusion | flops 100795392 | bytes 8913921 | tf_op jit(solution)/shard_map/while/body/eval_jaxpr/rgkt,rgkad->tad/dot_general | solution.py:53
  902.6 3.1 constant_dynamic-slice_fusion.9
  911.8 4.5 fusion.61
  916.3 14.6 %fusion.63 = f32[4,128,128]{2,0,1:T(4,128)S(1)} fusion(f32[4,4,8,128,128]{4,3,2,1,0:T(8,128)} %fusion.61, f32[4,128,128]{2,0,1:T(4,128)S(1)} %get-tuple-element.418, pred[]{:T(512)S(6)} %compare.3, f32[4,4,8]{2,0,1:T(4,128)S(1)} %fusion.62, s32[4,4,8]{2,0,1:T(4,128)S(1)} %get-tuple-element.402), kind=kOutput, calls=%fused_computation.14.clone.1 | convolution fusion | flops 100795392 | bytes 8913921 | tf_op jit(solution)/shard_map/while/body/eval_jaxpr/rgkt,rgkad->tad/dot_general | solution.py:53
  931.0 3.1 constant_dynamic-slice_fusion.9
  940.1 4.5 fusion.61
  944.7 14.6 %fusion.63 = f32[4,128,128]{2,0,1:T(4,128)S(1)} fusion(f32[4,4,8,128,128]{4,3,2,1,0:T(8,128)} %fusion.61, f32[4,128,128]{2,0,1:T(4,128)S(1)} %get-tuple-element.418, pred[]{:T(512)S(6)} %compare.3, f32[4,4,8]{2,0,1:T(4,128)S(1)} %fusion.62, s32[4,4,8]{2,0,1:T(4,128)S(1)} %get-tuple-element.402), kind=kOutput, calls=%fused_computation.14.clone.1 | convolution fusion | flops 100795392 | bytes 8913921 | tf_op jit(solution)/shard_map/while/body/eval_jaxpr/rgkt,rgkad->tad/dot_general | solution.py:53
  960.0 100.3 %all-reduce.2.cloned.1.call-done = f32[512,128]{1,0:T(8,128)} async-done(((f32[512,128]{1,0:T(8,128)}), f32[512,128]{1,0:T(8,128)}) %all-reduce.2.cloned.1.call-update) | async-done | bytes 262160 | tf_op jit(solution)/shard_map/psum | solution.py:79
  (163 shorter events, 83.0 us)
Async XLA Ops:
  6.5 1.0 copy-start
  33.5 448.9 %all-to-all-start.1 = ((bf16[64,4,512,128]{3,2,1,0:T(8,128)(2,1)}), bf16[64,4,512,128]{3,2,1,0:T(8,128)(2,1)}, u32[]{:S(2)}, u32[]{:S(2)}) async-start(bf16[64,4,512,128]{3,2,1,0:T(8,128)(2,1)} %stack.5), calls=%async_computation.1 | async-start | bytes 67108864 | tf_op jit(solution)/shard_map/all_to_all | solution.py:63
  44.1 1016.2 %all-reduce.2.cloned.1.call-start = ((), (), s32[]{:S(2)}) async-start(), calls=%async_computation.2 | async-start | bytes 524288 | tf_op jit(solution)/shard_map/psum | solution.py:79
  44.1 7.4 copy-start.5
  44.1 7.5 copy-start.6
  44.1 7.6 copy-start.7
  44.2 7.7 copy-start.8
  505.3 555.0 %copy-start.3 = (bf16[1,1,256,128]{3,2,1,0:T(8,128)(2,1)S(1)}, bf16[1,1,256,128]{3,2,1,0:T(8,128)(2,1)}, u32[]{:S(2)}) copy-start(bf16[1,1,256,128]{3,2,1,0:T(8,128)(2,1)} %param.10) | copy-start | bytes 196612
  505.3 555.0 %copy-start.4 = (bf16[128,128]{1,0:T(8,128)(2,1)S(1)}, bf16[128,128]{1,0:T(8,128)(2,1)}, u32[]{:S(2)}) copy-start(bf16[128,128]{1,0:T(8,128)(2,1)} %param.12) | copy-start | bytes 98308
  511.1 2.2 copy-start.2
  539.5 2.2 copy-start.2
  567.8 2.2 copy-start.2
  596.2 2.2 copy-start.2
  624.6 2.2 copy-start.2
  652.9 2.2 copy-start.2
  681.3 2.2 copy-start.2
  709.7 2.2 copy-start.2
  738.1 2.2 copy-start.2
  766.4 2.2 copy-start.2
  794.8 2.2 copy-start.2
  823.2 2.2 copy-start.2
  851.5 2.2 copy-start.2
  879.9 2.2 copy-start.2
  908.3 2.2 copy-start.2
  936.6 2.2 copy-start.2
  959.3 102.7 %copy-start.1 = (bf16[8,128,128]{2,1,0:T(8,128)(2,1)S(1)}, bf16[8,128,128]{2,1,0:T(8,128)(2,1)}, u32[]{:S(2)}) copy-start(bf16[8,128,128]{2,1,0:T(8,128)(2,1)} %param.11) | copy-start | bytes 786436
Sparse Core Ops, SparseCore 0:
  960.2 100.0 all-reduce.1
